TPU v7x, 32 devices: a whole 2x2x4 slice. The times are simulated.
32 devices in a mesh: member: 2 (over x), wave: 16 (over z, y, core).
Axes of the slice: x: 2, y: 2, z: 4, core: 2. Of those that a mesh axis runs over, the one named last changes fastest.
Arguments:
- spectral: bfloat16 [1024, 2, 256, 192], P(('member', 'wave')), parts along dimension 0, may hold values from -6 to 6
- basis: bfloat16 [512, 2, 256, 256], P('wave'), may hold values from -0.25 to 0.25
- quad_weights: float32 [256], replicated, may hold values from 0.5 to 2
- column: float32 [96, 96], replicated, may hold values from -0.625 to 0.625
- square_coef: float32 [96], replicated, may hold values from -0.3 to 0.3
- cube_coef: float32 [96], replicated, may hold values from 0.05 to 0.2
- trunc: int32 [256], replicated, may hold values from 16 to 512, as said below
Outputs:
- new_spectral: bfloat16 [1024, 2, 256, 192], P(('member', 'wave')), parts along dimension 0
There are 2 independent parts, one for each index of `member`. A program takes and returns all parts, laid end to end along the dimension named above; an argument that names none is the same for every part. Nothing has to cross between parts.
Inputs may be any that keep to these rules, and one draw needn't show every extreme that they name: `trunc`: rows nearer the equator never keep fewer wavenumbers than rows nearer the pole.
All inputs are finite; a program needn't handle non-finite values.
Results may differ from a plain program's by a relative error of at most 0.0057.
Values may be sent and summed in bfloat16 or wider, within the bound.
No kernel may reach another device: no remote copies, remote signals or barrier semaphores. Data moves between devices by JAX's collectives and lax.ppermute only.
A program may use at most 128 MiB of HBM per device.

v0:
```python
import math
import jax
import jax.numpy as jnp
from jax import lax
from jax.sharding import PartitionSpec as P

NLON = 1024


def fourier_table(wave_count, lon_count):
    wave_ids = jnp.arange(wave_count, dtype=jnp.int32)
    lon_ids = jnp.arange(lon_count, dtype=jnp.int32)
    phases = wave_ids[:, None] * lon_ids[None, :] % NLON
    angles = phases.astype(jnp.float32) * (2.0 * math.pi / NLON)
    return jnp.stack([jnp.cos(angles), -jnp.sin(angles)], axis=1).astype(jnp.bfloat16)


def per_device(spectral, basis, quad_weights, column, square_coef, cube_coef, trunc):
    devices = lax.axis_size("wave")
    position = lax.axis_index("wave")
    local_waves = spectral.shape[0]
    half_slots = spectral.shape[2]
    channels = spectral.shape[3]
    levels = channels // 2
    half_lats = basis.shape[3]
    wave_ids = position * local_waves + jnp.arange(local_waves, dtype=jnp.int32)
    degrees = (
        wave_ids[:, None, None]
        + 2 * jnp.arange(half_slots, dtype=jnp.int32)[None, None, :]
        + jnp.arange(2, dtype=jnp.int32)[None, :, None]
    )
    in_range = (degrees < 2 * half_slots)[..., None]
    spec_in = jnp.where(in_range, spectral, jnp.zeros_like(spectral))
    parities = jnp.einsum("mpkj,mpkc->mpjc", basis, spec_in, preferred_element_type=jnp.float32)
    north_rows = parities[:, 0] + parities[:, 1]
    south_rows = parities[:, 0] - parities[:, 1]
    pair_rows = half_lats // devices
    pair_lats = position * pair_rows + jnp.arange(pair_rows, dtype=jnp.int32)
    packed = jnp.stack([north_rows, south_rows], axis=1).astype(jnp.bfloat16)
    arrived = lax.all_to_all(packed, "wave", split_axis=2, concat_axis=0, tiled=True)
    coeffs = arrived.reshape(arrived.shape[0], 2 * pair_rows, channels)
    row_lats = jnp.concatenate([pair_lats, pair_lats])
    total_waves = coeffs.shape[0]
    grid_rows = coeffs.shape[1]
    trunc_rows = trunc[row_lats]
    weight_rows = quad_weights[row_lats]
    kept_mask = (jnp.arange(total_waves, dtype=jnp.int32)[:, None] < trunc_rows[None, :])[..., None]
    coeffs = jnp.where(kept_mask, coeffs, jnp.zeros_like(coeffs))
    coeff_four = coeffs.reshape(total_waves, grid_rows, 2, levels)
    fourier = fourier_table(total_waves, NLON)
    grid_temp = jnp.einsum("mgrv,mrx->gvx", coeff_four, fourier, preferred_element_type=jnp.float32)
    grid_temp = grid_temp * (1.0 / math.sqrt(total_waves))
    column_mix = jnp.einsum("uv,gvx->gux", column, grid_temp, precision=lax.Precision.HIGHEST)
    tendency = (
        column_mix
        + square_coef[None, :, None] * grid_temp * grid_temp
        - cube_coef[None, :, None] * grid_temp * grid_temp * grid_temp
    )
    partial_sum = jnp.sum(tendency * weight_rows[:, None, None], axis=(0, 2))
    level_total = lax.psum(partial_sum, "wave")
    level_mean = level_total / (NLON * 2.0 * jnp.sum(quad_weights))
    shifted = (tendency - level_mean[None, :, None]).astype(jnp.bfloat16)
    analysed = jnp.einsum(
        "gvx,mrx->mgrv", shifted, fourier, preferred_element_type=jnp.float32
    ) * math.sqrt(2.0 / NLON)
    analysed = analysed.reshape(total_waves, grid_rows, channels)
    analysed = jnp.where(kept_mask, analysed, 0.0).astype(jnp.bfloat16)
    settled = lax.optimization_barrier(analysed).astype(jnp.float32)
    north_back = settled[:, :pair_rows]
    south_back = settled[:, pair_rows:]
    weight = quad_weights[pair_lats][None, :, None]
    folded_part = jnp.stack(
        [weight * (north_back + south_back), weight * (north_back - south_back)], axis=1
    ).astype(jnp.bfloat16)
    folded = lax.all_to_all(folded_part, "wave", split_axis=0, concat_axis=2, tiled=True)
    direct = jnp.einsum("mpkj,mpjc->mpkc", basis, folded, preferred_element_type=jnp.float32)
    return jnp.where(in_range, spec_in.astype(jnp.float32) + direct, 0.0).astype(jnp.bfloat16)


def solution(mesh):
    return jax.shard_map(
        per_device,
        mesh=mesh,
        in_specs=(
            P(("member", "wave"), None, None, None),
            P("wave", None, None, None),
            P(),
            P(),
            P(),
            P(),
            P(),
        ),
        out_specs=P(("member", "wave"), None, None, None),
        check_vma=False,
    )
```

profile of v0, /device:TPU:1, one launch (start us, length us, event | category | flops | bytes accessed | tf_op | source)
XLA Modules:
  0.0 613.8 jit_solution(11071485273975315123)
XLA Ops:
  0.0 0.0 copy-start
  0.0 0.1 broadcast_add_fusion
  0.1 7.0 %fusion.14 = f32[32,2,256,192]{2,3,1,0:T(8,128)S(1)} fusion(bf16[32,2,256,256]{3,2,1,0:T(8,128)(2,1)} %param.8, bf16[32,2,256,192]{2,3,1,0:T(8,128)(2,1)} %param.7, pred[32,2,256]{2,1,0:T(4,128)(4,1)S(1)} %add_compare_fusion), kind=kOutput, calls=%fused_computation.34 | convolution fusion | flops 1613758464 | bytes 27279360 | tf_op jit(solution)/shard_map/mpkj,mpkc->mpjc/dot_general | solution.py:34
  7.2 2.7 add_convert_fusion
  9.8 5.2 pad_maximum_fusion
  15.0 21.1 %copy.19 = bf16[32,2,256,192]{3,1,0,2:T(2,128)(2,1)} copy(bf16[32,2,256,192]{2,3,1,0:T(8,128)(2,1)} %pad_maximum_fusion) | data formatting | bytes 12582912 | tf_op jit(solution)/shard_map/stack | solution.py:39
  36.1 7.9 %all-to-all-start = ((bf16[32,2,256,192]{3,1,0,2:T(2,128)(2,1)}), bf16[32,2,256,192]{3,1,0,2:T(2,128)(2,1)}, u32[]{:S(2)}, u32[]{:S(2)}) async-start(bf16[32,2,256,192]{3,1,0,2:T(2,128)(2,1)} %copy.19), calls=%async_computation | async-start | bytes 16777216 | tf_op jit(solution)/shard_map/all_to_all | solution.py:40
  44.1 0.6 reduce_sum.19
  44.7 0.1 fusion.30
  44.8 0.7 gather_fusion.2
  45.5 0.7 gather_fusion.1
  46.2 0.7 gather_fusion
  46.9 0.1 copy.18
  47.7 8.5 %negate_convert_fusion = (bf16[512,1,1024]{2,0,1:T(8,128)(2,1)S(1)}, bf16[512,1,1024]{2,0,1:T(8,128)(2,1)S(1)}) fusion(), kind=kLoop, calls=%fused_computation.47 | loop fusion | flops 8912896 | bytes 2097152 | tf_op jit(solution)/shard_map/convert.7
  56.2 138.8 %all-to-all-done = bf16[32,2,256,192]{3,1,0,2:T(2,128)(2,1)} async-done(((bf16[32,2,256,192]{3,1,0,2:T(2,128)(2,1)}), bf16[32,2,256,192]{3,1,0,2:T(2,128)(2,1)}, u32[]{:S(2)}, u32[]{:S(2)}) %all-to-all-start) | async-done | bytes 6291488 | tf_op jit(solution)/shard_map/all_to_all | solution.py:40
  195.1 13.4 %copy.20 = bf16[32,2,256,192]{3,2,1,0:T(8,128)(2,1)} copy(bf16[32,2,256,192]{3,1,0,2:T(2,128)(2,1)} %all-to-all-done) | data formatting | bytes 12582912 | tf_op jit(solution)/shard_map/all_to_all | solution.py:40
  208.5 7.9 %copy.21 = bf16[16,32,2,16,192]{4,3,2,1,0:T(8,128)(2,1)} copy(bf16[16,32,2,16,192]{4,3,0,2,1:T(8,128)(2,1)} %bitcast.75) | data formatting | bytes 12582912 | tf_op jit(solution)/shard_map/all_to_all | solution.py:40
  216.4 13.8 %reshape.210 = bf16[512,32,2,96]{3,2,1,0:T(2,128)(2,1)} reshape(bf16[16,32,2,16,192]{4,3,2,1,0:T(8,128)(2,1)} %copy.21) | data formatting | bytes 12582912 | tf_op jit(solution)/shard_map/reshape | solution.py:41
  230.2 23.7 %broadcast_select_fusion = bf16[512,32,2,96]{3,2,1,0:T(2,128)(2,1)S(1)} fusion(bf16[512,32,2,96]{3,2,1,0:T(2,128)(2,1)} %reshape.210, pred[512,32]{1,0:T(8,128)(4,1)S(1)} %iota_compare_fusion), kind=kLoop, calls=%fused_computation.4 | loop fusion | flops 3145728 | bytes 12599296 | tf_op jit(solution)/shard_map/jit(_where)/select_n | solution.py:48
  253.9 26.1 %fusion.6 = f32[32,96,1024,1]{2,1,3,0:T(8,128)} fusion(bf16[512,32,2,96]{3,2,1,0:T(2,128)(2,1)S(1)} %broadcast_select_fusion, bf16[512,1,1024]{2,0,1:T(8,128)(2,1)S(1)} %get-tuple-element.11, bf16[512,1,1024]{2,0,1:T(8,128)(2,1)S(1)} %get-tuple-element.12), kind=kOutput, calls=%fused_computation.20 | convolution fusion | flops 6443499520 | bytes 20971520 | tf_op jit(solution)/shard_map/mgrv,mrx->gvx/dot_general | solution.py:51
  280.0 25.0 %multiply_reduce_fusion = (f32[96]{0:T(128)S(1)}, f32[32,96,1024]{2,1,0:T(8,128)}) fusion(f32[32]{0:T(128)S(1)} %gather_fusion.2, f32[96]{0:T(128)S(1)} %get-tuple-element.13, f32[96]{0:T(128)S(1)} %get-tuple-element.14, f32[32,96,1024,1]{2,1,3,0:T(8,128)} %fusion.6, f32[96,96]{1,0:T(8,128)S(1)} %copy-done), kind=kOutput, calls=%fused_computation.19 | convolution fusion | flops 3658481664 | bytes 25203968 | tf_op jit(solution)/shard_map/uv,gvx->gux/dot_general | solution.py:53
  305.1 59.4 %psum.7 = f32[96]{0:T(128)S(1)} all-reduce(f32[96]{0:T(128)S(1)} %get-tuple-element.9), channel_id=1, replica_groups=mesh['member'=2,'wave'=16] {'wave'}, use_global_device_ids=true, to_apply=%region_1.2 | all-reduce | flops 96 | bytes 768 | tf_op jit(solution)/shard_map/psum | solution.py:60
  364.5 12.2 %multiply_bitcast_fusion = bf16[512,32,2,96]{0,3,1,2:T(8,128)(2,1)S(1)} fusion(f32[32,96,1024]{2,1,0:T(8,128)} %get-tuple-element.10, f32[96]{0:T(128)S(1)} %broadcast_divide_fusion, bf16[512,1,1024]{2,0,1:T(8,128)(2,1)S(1)} %get-tuple-element.11, bf16[512,1,1024]{2,0,1:T(8,128)(2,1)S(1)} %get-tuple-element.12), kind=kOutput, calls=%fused_computation.17 | convolution fusion | flops 6459228160 | bytes 20971904 | tf_op jit(solution)/shard_map/gvx,mrx->mgrv/dot_general | solution.py:63
  376.7 0.7 copy.23
  377.4 2.2 fusion.3
  379.6 1.7 convert_element_type.38
  381.3 2.7 fusion.17
  384.0 3.2 pad_maximum_fusion.1
  387.2 14.2 %copy.24 = bf16[512,2,16,192]{3,2,1,0:T(8,128)(2,1)} copy(bf16[512,2,16,192]{0,3,2,1:T(8,128)(2,1)} %pad_maximum_fusion.1) | data formatting | bytes 12582912 | tf_op jit(solution)/shard_map/stack | solution.py:72
  401.4 192.1 %all_to_all.33 = bf16[512,2,16,192]{3,2,1,0:T(8,128)(2,1)} all-to-all(bf16[512,2,16,192]{3,2,1,0:T(8,128)(2,1)} %copy.24), channel_id=1, replica_groups=mesh['member'=2,'wave'=16] {'wave'}, dimensions={0} | all-to-all | bytes 12582912 | tf_op jit(solution)/shard_map/all_to_all | solution.py:75
  593.5 7.8 %copy.25 = bf16[32,2,16,16,192]{4,3,2,1,0:T(8,128)(2,1)} copy(bf16[32,2,16,16,192]{4,3,1,0,2:T(8,128)(2,1)} %bitcast.76) | data formatting | bytes 12582912 | tf_op jit(solution)/shard_map/all_to_all | solution.py:75
  601.3 12.3 %fusion.2 = bf16[32,2,256,192]{2,3,1,0:T(8,128)(2,1)} fusion(pred[32,2,256]{2,1,0:T(4,128)(4,1)S(1)} %add_compare_fusion, bf16[32,2,256,192]{2,3,1,0:T(8,128)(2,1)} %param.7, bf16[32,2,256,192]{3,2,1,0:T(8,128)(2,1)} %bitcast.77, bf16[32,2,256,256]{3,2,1,0:T(8,128)(2,1)} %param.8), kind=kOutput, calls=%fused_computation.8 | convolution fusion | flops 1626341376 | bytes 27279360 | tf_op jit(solution)/shard_map/mpkj,mpjc->mpkc/dot_general | solution.py:76
  (21 shorter events, 0.2 us)
Async XLA Ops:
  0.0 280.0 %copy-start = (f32[96,96]{1,0:T(8,128)S(1)}, f32[96,96]{1,0:T(8,128)}, u32[]{:S(2)}) copy-start(f32[96,96]{1,0:T(8,128)} %param.10) | copy-start | bytes 110596
  36.1 8.0 %copy-start.2 = (f32[256]{0:T(256)S(1)}, f32[256]{0:T(256)}, u32[]{:S(2)}) copy-start(f32[256]{0:T(256)} %param.9) | copy-start | bytes 3076
  36.1 9.4 %copy-start.3 = (s32[256]{0:T(256)S(1)}, s32[256]{0:T(256)}, u32[]{:S(2)}) copy-start(s32[256]{0:T(256)} %param.13) | copy-start | bytes 3076
  36.1 11.6 %copy-start.4 = (f32[96]{0:T(128)S(1)}, f32[96]{0:T(128)}, u32[]{:S(2)}) copy-start(f32[96]{0:T(128)} %param.12) | copy-start | bytes 1156
  36.1 11.6 %copy-start.5 = (f32[96]{0:T(128)S(1)}, f32[96]{0:T(128)}, u32[]{:S(2)}) copy-start(f32[96]{0:T(128)} %param.11) | copy-start | bytes 1156
  36.1 158.9 %all-to-all-start = ((bf16[32,2,256,192]{3,1,0,2:T(2,128)(2,1)}), bf16[32,2,256,192]{3,1,0,2:T(2,128)(2,1)}, u32[]{:S(2)}, u32[]{:S(2)}) async-start(bf16[32,2,256,192]{3,1,0,2:T(2,128)(2,1)} %copy.19), calls=%async_computation | async-start | bytes 16777216 | tf_op jit(solution)/shard_map/all_to_all | solution.py:40
  601.3 12.3 %copy-start.1 = (f32[96,96]{1,0:T(8,128)S(1)}, f32[96,96]{1,0:T(8,128)}, u32[]{:S(2)}) copy-start(f32[96,96]{1,0:T(8,128)} %param.10) | copy-start | bytes 110596
where the time goes:
time: 619 us; the launch traced here: 614 us
  blocking collectives  251 us (41%)
  waiting for transfers between devices  139 us (22%)
  matrix products  82.6 us (13%)
  local copies, waits for them, and re-layouts  81.2 us (13%)
  other arithmetic  50.7 us (8%)
  starting transfers between devices  7.92 us (1%)
    all_to_all x1, blocking collectives, per_device(): lax.all_to_all(folded_part, 'wave', split_axis=0, concat_axis=2, tiled=True)  192 us
    all_to_all x1, waiting for transfers between devices, per_device(): lax.all_to_all(packed, 'wave', split_axis=2, concat_axis=0, tiled=True)  139 us
    psum x1, blocking collectives, per_device(): level_total = lax.psum(partial_sum, 'wave')  59.4 us
    dot_general x1, matrix products, per_device(): jnp.einsum('mgrv,mrx->gvx', coeff_four, fourier, preferred_element_type=j...  26.1 us
    dot_general x1, matrix products, per_device(): jnp.einsum('uv,gvx->gux', column, grid_temp, precision=lax.Precision.HIGH...  25 us
    select_n x1, other arithmetic, per_device(): coeffs = jnp.where(kept_mask, coeffs, jnp.zeros_like(coeffs))  23.7 us
    all_to_all x2, local copies, waits for them, and re-layouts, per_device(): lax.all_to_all(packed, 'wave', split_axis=2, concat_axis=0, tiled=True)  21.4 us
    another operation x1, local copies, waits for them, and re-layouts, per_device(): packed = jnp.stack([north_rows, south_rows], axis=1).astype(jnp.bfloat16)  21.1 us
  transfers between devices with their start and end apart: 1, of which 1 were waited for; matrix products, arithmetic and copies ran while one was open for 2% of the time, Pallas kernels for 0%

commit v1 on v0

--- a/solution.py
+++ b/solution.py
@@ -5,6 +5,15 @@
 from jax.sharding import PartitionSpec as P
 
 NLON = 1024
+
+
+def add_in_pairs(x, mesh_axis):
+    size = lax.axis_size(mesh_axis)
+    result, far = (x, 1)
+    while far < size:
+        result = result + lax.ppermute(result, mesh_axis, [(i, i ^ far) for i in range(size)])
+        far = 2 * far
+    return result
 
 
 def fourier_table(wave_count, lon_count):
@@ -57,7 +66,7 @@
         - cube_coef[None, :, None] * grid_temp * grid_temp * grid_temp
     )
     partial_sum = jnp.sum(tendency * weight_rows[:, None, None], axis=(0, 2))
-    level_total = lax.psum(partial_sum, "wave")
+    level_total = add_in_pairs(partial_sum, "wave")
     level_mean = level_total / (NLON * 2.0 * jnp.sum(quad_weights))
     shifted = (tendency - level_mean[None, :, None]).astype(jnp.bfloat16)
     analysed = jnp.einsum(

time: 619 us -> 599 us (0.968)
  blocking collectives: 251 us -> 190 us
  starting transfers between devices: 7.92 us -> 44.6 us
    psum x1 -> x0, blocking collectives: 59.4 us -> none  [per_device(): level_total = lax.psum(partial_sum, 'wave')]
    ppermute x0 -> x4, starting transfers between devices: none -> 36.7 us  [add_in_pairs(): lax.ppermute(result, mesh_axis, [(i, i ^ far) for i in range(size)])]
  transfers between devices with their start and end apart: 1 -> 5, of which waited for: 1 -> 4; matrix products, arithmetic and copies ran while one was open for 2% -> 2% of each run, Pallas kernels for 0% -> 0%
where the time goes in v1:
time: 599 us; the launch traced here: 594 us
  blocking collectives  190 us (32%)
  waiting for transfers between devices  144 us (24%)
  matrix products  82.9 us (14%)
  local copies, waits for them, and re-layouts  81.1 us (14%)
  other arithmetic  50.7 us (8%)
  starting transfers between devices  44.6 us (7%)
    all_to_all x1, blocking collectives, per_device(): lax.all_to_all(folded_part, 'wave', split_axis=0, concat_axis=2, tiled=True)  190 us
    all_to_all x1, waiting for transfers between devices, per_device(): lax.all_to_all(packed, 'wave', split_axis=2, concat_axis=0, tiled=True)  141 us
    ppermute x4, starting transfers between devices, add_in_pairs(): lax.ppermute(result, mesh_axis, [(i, i ^ far) for i in range(size)])  36.7 us
    dot_general x1, matrix products, per_device(): jnp.einsum('mgrv,mrx->gvx', coeff_four, fourier, preferred_element_type=j...  26.1 us
    dot_general x1, matrix products, per_device(): jnp.einsum('uv,gvx->gux', column, grid_temp, precision=lax.Precision.HIGH...  25.1 us
    select_n x1, other arithmetic, per_device(): coeffs = jnp.where(kept_mask, coeffs, jnp.zeros_like(coeffs))  23.7 us
    all_to_all x2, local copies, waits for them, and re-layouts, per_device(): lax.all_to_all(packed, 'wave', split_axis=2, concat_axis=0, tiled=True)  21.4 us
    another operation x1, local copies, waits for them, and re-layouts, per_device(): packed = jnp.stack([north_rows, south_rows], axis=1).astype(jnp.bfloat16)  21 us
  transfers between devices with their start and end apart: 5, of which 4 were waited for; matrix products, arithmetic and copies ran while one was open for 2% of the time, Pallas kernels for 0%

profile of v1, /device:TPU:1, one launch (start us, length us, event | category | flops | bytes accessed | tf_op | source)
XLA Modules:
  0.0 594.4 jit_solution(2933941471523115061)
XLA Ops:
  0.1 7.0 %fusion.14 = f32[32,2,256,192]{2,3,1,0:T(8,128)S(1)} fusion(bf16[32,2,256,256]{3,2,1,0:T(8,128)(2,1)} %param.8, bf16[32,2,256,192]{2,3,1,0:T(8,128)(2,1)} %param.7, pred[32,2,256]{2,1,0:T(4,128)(4,1)S(1)} %add_compare_fusion), kind=kOutput, calls=%fused_computation.34 | convolution fusion | flops 1613758464 | bytes 27279360 | tf_op jit(solution)/shard_map/mpkj,mpkc->mpjc/dot_general | solution.py:43
  7.2 2.7 add_convert_fusion
  9.8 5.2 pad_maximum_fusion
  15.0 21.0 %copy.19 = bf16[32,2,256,192]{3,1,0,2:T(2,128)(2,1)} copy(bf16[32,2,256,192]{2,3,1,0:T(8,128)(2,1)} %pad_maximum_fusion) | data formatting | bytes 12582912 | tf_op jit(solution)/shard_map/stack | solution.py:48
  36.0 7.9 %all-to-all-start = ((bf16[32,2,256,192]{3,1,0,2:T(2,128)(2,1)}), bf16[32,2,256,192]{3,1,0,2:T(2,128)(2,1)}, u32[]{:S(2)}, u32[]{:S(2)}) async-start(bf16[32,2,256,192]{3,1,0,2:T(2,128)(2,1)} %copy.19), calls=%async_computation | async-start | bytes 16777216 | tf_op jit(solution)/shard_map/all_to_all | solution.py:49
  44.1 0.7 gather_fusion.2
  44.8 0.7 gather_fusion.1
  45.6 8.5 %negate_convert_fusion = (bf16[512,1,1024]{2,0,1:T(8,128)(2,1)S(1)}, bf16[512,1,1024]{2,0,1:T(8,128)(2,1)S(1)}) fusion(), kind=kLoop, calls=%fused_computation.47 | loop fusion | flops 8912896 | bytes 2097152 | tf_op jit(solution)/shard_map/convert.7
  54.1 140.9 %all-to-all-done = bf16[32,2,256,192]{3,1,0,2:T(2,128)(2,1)} async-done(((bf16[32,2,256,192]{3,1,0,2:T(2,128)(2,1)}), bf16[32,2,256,192]{3,1,0,2:T(2,128)(2,1)}, u32[]{:S(2)}, u32[]{:S(2)}) %all-to-all-start) | async-done | bytes 6291488 | tf_op jit(solution)/shard_map/all_to_all | solution.py:49
  195.0 13.5 %copy.20 = bf16[32,2,256,192]{3,2,1,0:T(8,128)(2,1)} copy(bf16[32,2,256,192]{3,1,0,2:T(2,128)(2,1)} %all-to-all-done) | data formatting | bytes 12582912 | tf_op jit(solution)/shard_map/all_to_all | solution.py:49
  208.5 7.9 %copy.21 = bf16[16,32,2,16,192]{4,3,2,1,0:T(8,128)(2,1)} copy(bf16[16,32,2,16,192]{4,3,0,2,1:T(8,128)(2,1)} %bitcast.75) | data formatting | bytes 12582912 | tf_op jit(solution)/shard_map/all_to_all | solution.py:49
  216.4 13.8 %reshape.210 = bf16[512,32,2,96]{3,2,1,0:T(2,128)(2,1)} reshape(bf16[16,32,2,16,192]{4,3,2,1,0:T(8,128)(2,1)} %copy.21) | data formatting | bytes 12582912 | tf_op jit(solution)/shard_map/reshape | solution.py:50
  230.1 23.7 %broadcast_select_fusion = bf16[512,32,2,96]{3,2,1,0:T(2,128)(2,1)S(1)} fusion(bf16[512,32,2,96]{3,2,1,0:T(2,128)(2,1)} %reshape.210, pred[512,32]{1,0:T(8,128)(4,1)S(1)} %iota_compare_fusion), kind=kLoop, calls=%fused_computation.4 | loop fusion | flops 3145728 | bytes 12599296 | tf_op jit(solution)/shard_map/jit(_where)/select_n | solution.py:57
  253.9 26.1 %fusion.6 = f32[32,96,1024,1]{2,1,3,0:T(8,128)} fusion(bf16[512,32,2,96]{3,2,1,0:T(2,128)(2,1)S(1)} %broadcast_select_fusion, bf16[512,1,1024]{2,0,1:T(8,128)(2,1)S(1)} %get-tuple-element.11, bf16[512,1,1024]{2,0,1:T(8,128)(2,1)S(1)} %get-tuple-element.12), kind=kOutput, calls=%fused_computation.20 | convolution fusion | flops 6443499520 | bytes 20971520 | tf_op jit(solution)/shard_map/mgrv,mrx->gvx/dot_general | solution.py:60
  279.9 25.1 %multiply_reduce_fusion = (f32[96]{0:T(128)S(1)}, f32[32,96,1024]{2,1,0:T(8,128)}) fusion(f32[32]{0:T(128)S(1)} %gather_fusion.2, f32[96]{0:T(128)S(1)} %get-tuple-element.13, f32[96]{0:T(128)S(1)} %get-tuple-element.14, f32[32,96,1024,1]{2,1,3,0:T(8,128)} %fusion.6, f32[96,96]{1,0:T(8,128)S(1)} %copy-done), kind=kOutput, calls=%fused_computation.19 | convolution fusion | flops 3658481664 | bytes 25203968 | tf_op jit(solution)/shard_map/uv,gvx->gux/dot_general | solution.py:62
  305.1 1.1 collective-permute-done
  306.3 11.5 %collective-permute-start.1 = (f32[96]{0:T(128)S(1)}, f32[96]{0:T(128)S(1)}, u32[]{:S(2)}, u32[]{:S(2)}) collective-permute-start(f32[96]{0:T(128)S(1)} %add.165), channel_id=1, source_target_pairs={{0,2},{1,3},{2,0},{3,1},{4,6},{5,7},{6,4},{7,5},{8,10},{9,11},{10,... | collective-permute-start | bytes 1160 | tf_op jit(solution)/shard_map/ppermute | solution.py:14
  317.8 1.0 collective-permute-done.1
  318.8 22.2 %collective-permute-start.2 = (f32[96]{0:T(128)S(1)}, f32[96]{0:T(128)S(1)}, u32[]{:S(2)}, u32[]{:S(2)}) collective-permute-start(f32[96]{0:T(128)S(1)} %add.166), channel_id=1, source_target_pairs={{0,4},{1,5},{2,6},{3,7},{4,0},{5,1},{6,2},{7,3},{8,12},{9,13},{10,... | collective-permute-start | bytes 1160 | tf_op jit(solution)/shard_map/ppermute | solution.py:14
  341.0 0.9 collective-permute-done.2
  341.9 2.9 collective-permute-start.3
  345.5 0.7 gather_fusion
  346.9 12.5 %multiply_bitcast_fusion = bf16[512,32,2,96]{0,3,1,2:T(8,128)(2,1)S(1)} fusion(f32[32,96,1024]{2,1,0:T(8,128)} %get-tuple-element.10, f32[96]{0:T(128)S(1)} %add_divide_fusion, bf16[512,1,1024]{2,0,1:T(8,128)(2,1)S(1)} %get-tuple-element.11, bf16[512,1,1024]{2,0,1:T(8,128)(2,1)S(1)} %get-tuple-element.12), kind=kOutput, calls=%fused_computation.17 | convolution fusion | flops 6459228160 | bytes 20971904 | tf_op jit(solution)/shard_map/gvx,mrx->mgrv/dot_general | solution.py:72
  359.4 0.7 copy.23
  360.1 2.2 fusion.3
  362.3 1.7 convert_element_type.38
  364.0 2.7 fusion.17
  366.7 3.2 pad_maximum_fusion.1
  369.9 14.2 %copy.24 = bf16[512,2,16,192]{3,2,1,0:T(8,128)(2,1)} copy(bf16[512,2,16,192]{0,3,2,1:T(8,128)(2,1)} %pad_maximum_fusion.1) | data formatting | bytes 12582912 | tf_op jit(solution)/shard_map/stack | solution.py:81
  384.1 190.0 %all_to_all.33 = bf16[512,2,16,192]{3,2,1,0:T(8,128)(2,1)} all-to-all(bf16[512,2,16,192]{3,2,1,0:T(8,128)(2,1)} %copy.24), channel_id=1, replica_groups=mesh['member'=2,'wave'=16] {'wave'}, dimensions={0} | all-to-all | bytes 12582912 | tf_op jit(solution)/shard_map/all_to_all | solution.py:84
  574.1 7.9 %copy.25 = bf16[32,2,16,16,192]{4,3,2,1,0:T(8,128)(2,1)} copy(bf16[32,2,16,16,192]{4,3,1,0,2:T(8,128)(2,1)} %bitcast.76) | data formatting | bytes 12582912 | tf_op jit(solution)/shard_map/all_to_all | solution.py:84
  581.9 12.3 %fusion.2 = bf16[32,2,256,192]{2,3,1,0:T(8,128)(2,1)} fusion(pred[32,2,256]{2,1,0:T(4,128)(4,1)S(1)} %add_compare_fusion, bf16[32,2,256,192]{2,3,1,0:T(8,128)(2,1)} %param.7, bf16[32,2,256,192]{3,2,1,0:T(8,128)(2,1)} %bitcast.77, bf16[32,2,256,256]{3,2,1,0:T(8,128)(2,1)} %param.8), kind=kOutput, calls=%fused_computation.8 | convolution fusion | flops 1626341376 | bytes 27279360 | tf_op jit(solution)/shard_map/mpkj,mpjc->mpkc/dot_general | solution.py:85
  (31 shorter events, 1.1 us)
Async XLA Ops:
  0.0 279.9 %copy-start = (f32[96,96]{1,0:T(8,128)S(1)}, f32[96,96]{1,0:T(8,128)}, u32[]{:S(2)}) copy-start(f32[96,96]{1,0:T(8,128)} %param.10) | copy-start | bytes 110596
  36.0 8.0 %copy-start.2 = (f32[256]{0:T(256)S(1)}, f32[256]{0:T(256)}, u32[]{:S(2)}) copy-start(f32[256]{0:T(256)} %param.9) | copy-start | bytes 3076
  36.0 8.8 %copy-start.3 = (s32[256]{0:T(256)S(1)}, s32[256]{0:T(256)}, u32[]{:S(2)}) copy-start(s32[256]{0:T(256)} %param.13) | copy-start | bytes 3076
  36.0 9.5 %copy-start.4 = (f32[96]{0:T(128)S(1)}, f32[96]{0:T(128)}, u32[]{:S(2)}) copy-start(f32[96]{0:T(128)} %param.12) | copy-start | bytes 1156
  36.0 9.5 %copy-start.5 = (f32[96]{0:T(128)S(1)}, f32[96]{0:T(128)}, u32[]{:S(2)}) copy-start(f32[96]{0:T(128)} %param.11) | copy-start | bytes 1156
  36.0 158.9 %all-to-all-start = ((bf16[32,2,256,192]{3,1,0,2:T(2,128)(2,1)}), bf16[32,2,256,192]{3,1,0,2:T(2,128)(2,1)}, u32[]{:S(2)}, u32[]{:S(2)}) async-start(bf16[32,2,256,192]{3,1,0,2:T(2,128)(2,1)} %copy.19), calls=%async_computation | async-start | bytes 16777216 | tf_op jit(solution)/shard_map/all_to_all | solution.py:49
  305.1 1.2 collective-permute-start
  306.3 12.5 %collective-permute-start.1 = (f32[96]{0:T(128)S(1)}, f32[96]{0:T(128)S(1)}, u32[]{:S(2)}, u32[]{:S(2)}) collective-permute-start(f32[96]{0:T(128)S(1)} %add.165), channel_id=1, source_target_pairs={{0,2},{1,3},{2,0},{3,1},{4,6},{5,7},{6,4},{7,5},{8,10},{9,11},{10,... | collective-permute-start | bytes 1160 | tf_op jit(solution)/shard_map/ppermute | solution.py:14
  318.8 23.1 %collective-permute-start.2 = (f32[96]{0:T(128)S(1)}, f32[96]{0:T(128)S(1)}, u32[]{:S(2)}, u32[]{:S(2)}) collective-permute-start(f32[96]{0:T(128)S(1)} %add.166), channel_id=1, source_target_pairs={{0,4},{1,5},{2,6},{3,7},{4,0},{5,1},{6,2},{7,3},{8,12},{9,13},{10,... | collective-permute-start | bytes 1160 | tf_op jit(solution)/shard_map/ppermute | solution.py:14
  341.9 4.9 collective-permute-start.3
  581.9 12.3 %copy-start.1 = (f32[96,96]{1,0:T(8,128)S(1)}, f32[96,96]{1,0:T(8,128)}, u32[]{:S(2)}) copy-start(f32[96,96]{1,0:T(8,128)} %param.10) | copy-start | bytes 110596
